TPU v7x, 256 devices: a whole 4x4x8 slice. The times are simulated.
256 devices in a mesh: req: 8 (over y_hi, x), blk: 32 (over y_lo, z, core).
Axes of the slice: x: 4, y: 4 (y_hi: 2, y_lo: 2; y = y_hi * 2 + y_lo), z: 8, core: 2. Of those that a mesh axis runs over, the one named last changes fastest.
Arguments:
- prefill_resid: bfloat16 [1024, 2048], P(('blk', 'req')), may hold values from -3 to 3
- prefill_routes: int32 [1024, 6], P(('blk', 'req')), may hold values from 0 to 63, all different within a row; in each aligned block of 32 rows (0 to 31, 32 to 63, ...) at most 6 rows name the same one
- prefill_scores: float32 [1024, 6], P(('blk', 'req')), may hold values from 0.05 to 1
- decode_resid: bfloat16 [16, 2048], P('req'), may hold values from -3 to 3
- queries: bfloat16 [16, 16, 192], P('req'), may hold values from -8 to 8
- latent_cache: bfloat16 [16, 16384, 576], P('req', 'blk'), may hold values from -8 to 8
- new_latent: bfloat16 [16, 576], P('req'), may hold values from -8 to 8
- cache_lengths: int32 [16], P('req'), may hold values from 1 to 16384, 65536 in all
- decode_routes: int32 [16, 6], P('req'), may hold values from 0 to 63, all different within a row
- decode_scores: float32 [16, 6], P('req'), may hold values from 0.05 to 1
- norm_gain: float32 [2048], replicated, may hold values from 0.1 to 1.9
- absorb_key: bfloat16 [16, 128, 512], replicated, may hold values from -0.5 to 0.5
- absorb_value: bfloat16 [16, 512, 128], P('req'), may hold values from -6 to 6
- out_proj: bfloat16 [16, 128, 2048], P('req'), may hold values from -0.125 to 0.125
- expert_gate: bfloat16 [64, 2048, 1408], P('blk', None, 'req'), may hold values from -0.125 to 0.125
- expert_up: bfloat16 [64, 2048, 1408], P('blk', None, 'req'), may hold values from -0.125 to 0.125
- expert_down: bfloat16 [64, 1408, 2048], P('blk', 'req'), may hold values from -0.15625 to 0.15625
- shared_gate: bfloat16 [2048, 2816], P(None, 'req'), may hold values from -0.125 to 0.125
- shared_up: bfloat16 [2048, 2816], P(None, 'req'), may hold values from -0.125 to 0.125
- shared_down: bfloat16 [2816, 2048], P('req'), may hold values from -0.109375 to 0.109375
Outputs:
- prefill_out: bfloat16 [1024, 2048], P(('blk', 'req'))
- decode_out: bfloat16 [16, 2048], P('req')
Inputs may be any that keep to these rules, and one draw needn't show every extreme that they name: `prefill_routes`: each token names 6 different experts; every expert is named by some token; in each aligned block of 32 tokens no expert is named by more than 6 tokens, and in some block one expert is named by exactly 6. `decode_routes`: each decoded token names 6 different experts; every expert is named by some token. `cache_lengths`: some request has exactly 16384 cached positions.
All inputs are finite; a program needn't handle non-finite values. No bound on the sum of `cache_lengths` on one device may be relied on, other than what follows from the above.
Results may differ from a plain program's by a relative error of at most 0.02.
Values may be sent and summed in bfloat16 or wider, within the bound.
No kernel may reach another device: no remote copies, remote signals or barrier semaphores. Data moves between devices by JAX's collectives and lax.ppermute only.
A program may use at most 128 MiB of HBM per device.

v0:
```python
import jax
import jax.numpy as jnp
from jax import lax
from jax.sharding import PartitionSpec as P

NEG = -1e30
ROUTE_SCALE = 2.446


def merged(part, axis, combine):
    gathered = jax.tree.map(lambda a: lax.all_gather(a, axis), part)

    def take(source):
        return jax.tree.map(lambda a: lax.dynamic_index_in_dim(a, source, 0, False), gathered)

    return lax.fori_loop(
        1, lax.axis_size(axis), lambda source, state: combine(state, take(source)), take(0)
    )


def settle(values):
    return lax.optimization_barrier(values.astype(jnp.bfloat16)).astype(jnp.float32)


def rms_rows(rows_in, gain_row):
    widened = rows_in.astype(jnp.float32)
    mean_square = jnp.mean(widened * widened, axis=1, keepdims=True)
    return (widened * lax.rsqrt(mean_square + 1e-06) * gain_row).astype(jnp.bfloat16)


def swiglu(inputs, gate_w, up_w, down_w):
    gate_part = jnp.dot(inputs, gate_w, preferred_element_type=jnp.float32)
    up_part = jnp.dot(inputs, up_w, preferred_element_type=jnp.float32)
    hidden = (jax.nn.silu(gate_part) * up_part).astype(jnp.bfloat16)
    return jnp.dot(hidden, down_w, preferred_element_type=jnp.float32)


def gate_table(routes, scores, experts):
    shares = scores / jnp.sum(scores, axis=1, keepdims=True) * ROUTE_SCALE
    matches = routes[:, :, None] == jnp.arange(experts, dtype=jnp.int32)[None, None, :]
    return jnp.sum(jnp.where(matches, shares[:, :, None], 0.0), axis=1).astype(jnp.bfloat16)


def routed_terms(inputs, weight_rows, first_expert, gate_w, up_w, down_w):
    result = jnp.zeros(inputs.shape, jnp.float32)
    for slot_index in range(gate_w.shape[0]):
        weight_col = lax.dynamic_slice_in_dim(weight_rows, first_expert + slot_index, 1, 1).astype(
            jnp.float32
        )
        result = result + weight_col * swiglu(
            inputs, gate_w[slot_index], up_w[slot_index], down_w[slot_index]
        )
    return result


def merge_parts(first_part, second_part):
    row_peak = jnp.maximum(first_part[0], second_part[0])
    keep_first = jnp.exp(first_part[0] - row_peak)
    keep_second = jnp.exp(second_part[0] - row_peak)
    merged_total = first_part[1] * keep_first + second_part[1] * keep_second
    merged_sum = first_part[2] * keep_first[:, :, None] + second_part[2] * keep_second[:, :, None]
    return (row_peak, merged_total, merged_sum)


def local(
    prefill_resid,
    prefill_routes,
    prefill_scores,
    decode_resid,
    queries,
    latent_cache,
    new_latent,
    cache_lengths,
    decode_routes,
    decode_scores,
    norm_gain,
    absorb_key,
    absorb_value,
    out_proj,
    expert_gate,
    expert_up,
    expert_down,
    shared_gate,
    shared_up,
    shared_down,
):
    req_count = lax.axis_size("req")
    blk_count = lax.axis_size("blk")
    blk_index = lax.axis_index("blk")
    nope_width = absorb_key.shape[1]
    latent_width = absorb_key.shape[2]
    scale_factor = queries.shape[2] ** (-0.5)
    positions = latent_cache.shape[1]
    requests = queries.shape[0]
    head_count = queries.shape[1]
    q_latent = jnp.einsum(
        "ihn,hnl->ihl", queries[:, :, :nope_width], absorb_key, preferred_element_type=jnp.float32
    ).astype(jnp.bfloat16)
    q_full = jnp.concatenate([q_latent, queries[:, :, nope_width:]], axis=2)
    first_position = blk_index * positions
    live_mask = (first_position + jnp.arange(positions, dtype=jnp.int32))[None, :] < cache_lengths[
        :, None
    ]

    def local_part(operand):
        scores = (
            jnp.einsum("ihc,ipc->ihp", q_full, latent_cache, preferred_element_type=jnp.float32)
            * scale_factor
        )
        scores = jnp.where(live_mask[:, None, :], scores, NEG)
        row_peak = jnp.max(scores, axis=2)
        expo_weights = jnp.where(live_mask[:, None, :], jnp.exp(scores - row_peak[:, :, None]), 0.0)
        weighted = jnp.einsum(
            "ihp,ipl->ihl",
            expo_weights.astype(jnp.bfloat16),
            latent_cache[:, :, :latent_width],
            preferred_element_type=jnp.float32,
        )
        return (row_peak, jnp.sum(expo_weights, axis=2), weighted)

    def empty_part(operand):
        return (
            jnp.full((requests, head_count), NEG, jnp.float32),
            jnp.zeros((requests, head_count), jnp.float32),
            jnp.zeros((requests, head_count, latent_width), jnp.float32),
        )

    partials = lax.cond(jnp.max(cache_lengths) > first_position, local_part, empty_part, 0)
    row_peak, denominator, weighted = merged(partials, "blk", merge_parts)
    fresh_score = (
        jnp.einsum("ihc,ic->ih", q_full, new_latent, preferred_element_type=jnp.float32)
        * scale_factor
    )
    overall = jnp.maximum(row_peak, fresh_score)
    keep_old = jnp.exp(row_peak - overall)
    fresh_weight = jnp.exp(fresh_score - overall)
    denominator = denominator * keep_old + fresh_weight
    weighted = weighted * keep_old[:, :, None] + settle(fresh_weight)[:, :, None] * new_latent[
        :, None, :latent_width
    ].astype(jnp.float32)
    o_latent = (weighted / denominator[:, :, None]).astype(jnp.bfloat16)
    value_piece = lax.all_gather(absorb_value, "req", axis=0, tiled=True)
    proj_piece = lax.all_gather(out_proj, "req", axis=0, tiled=True)
    head_values = jnp.einsum(
        "ihl,hlv->ihv", o_latent, value_piece, preferred_element_type=jnp.float32
    ).astype(jnp.bfloat16)
    attention = jnp.einsum(
        "ihv,hvd->id", head_values, proj_piece, preferred_element_type=jnp.float32
    )
    hidden_dec = (decode_resid.astype(jnp.float32) + attention).astype(jnp.bfloat16)
    experts = expert_gate.shape[0] * blk_count
    first_expert = blk_index * expert_gate.shape[0]
    own_rows = jnp.concatenate(
        [rms_rows(prefill_resid, norm_gain), rms_rows(hidden_dec, norm_gain)], axis=0
    )
    own_table = jnp.concatenate(
        [
            gate_table(prefill_routes, prefill_scores, experts),
            gate_table(decode_routes, decode_scores, experts),
        ],
        axis=0,
    )
    tile_rows = own_rows.shape[0]
    model_width = own_rows.shape[1]
    every_rows, every_table = (
        lax.all_gather(own_rows, ("req", "blk"), axis=0, tiled=True),
        lax.all_gather(own_table, ("req", "blk"), axis=0, tiled=True),
    )
    grid_rows = every_rows.reshape(req_count, blk_count, tile_rows, model_width)
    column_rows = lax.dynamic_index_in_dim(grid_rows, blk_index, 1, keepdims=False).reshape(
        req_count * tile_rows, model_width
    )
    shared_column = swiglu(column_rows, shared_gate, shared_up, shared_down).reshape(
        req_count, tile_rows, model_width
    )
    routed = routed_terms(
        every_rows, every_table, first_expert, expert_gate, expert_up, expert_down
    )
    tile_ids = jnp.arange(tile_rows * lax.axis_size(("req", "blk")) // tile_rows, dtype=jnp.int32)
    in_column = tile_ids % blk_count == blk_index
    owner_rows = (tile_ids // blk_count)[:, None] == jnp.arange(req_count, dtype=jnp.int32)[None, :]
    selector = jnp.logical_and(in_column[:, None], owner_rows).astype(jnp.float32)
    shared_part = jnp.einsum(
        "tr,rnd->tnd", selector, shared_column, precision=lax.Precision.HIGHEST
    )
    moe_rows = lax.psum_scatter(
        routed + shared_part.reshape(tile_rows * lax.axis_size(("req", "blk")), model_width),
        ("req", "blk"),
        scatter_dimension=0,
        tiled=True,
    )
    prefill_count = prefill_resid.shape[0]
    prefill_out = (prefill_resid.astype(jnp.float32) + moe_rows[:prefill_count]).astype(
        jnp.bfloat16
    )
    decode_out = (hidden_dec.astype(jnp.float32) + moe_rows[prefill_count:]).astype(jnp.bfloat16)
    return (prefill_out, decode_out)


def solution(mesh):
    return jax.shard_map(
        local,
        mesh=mesh,
        in_specs=(
            P(("blk", "req"), None),
            P(("blk", "req"), None),
            P(("blk", "req"), None),
            P("req", None),
            P("req", None, None),
            P("req", "blk", None),
            P("req", None),
            P("req"),
            P("req", None),
            P("req", None),
            P(),
            P(),
            P("req", None, None),
            P("req", None, None),
            P("blk", None, "req"),
            P("blk", None, "req"),
            P("blk", "req", None),
            P(None, "req"),
            P(None, "req"),
            P("req", None),
        ),
        out_specs=(P(("blk", "req"), None), P("req", None)),
        check_vma=False,
    )
```

profile of v0, /device:TPU:8, one launch (start us, length us, event | category | flops | bytes accessed | tf_op | source)
XLA Modules:
  0.0 1075.9 jit_solution(22341837289912471)
XLA Ops:
  8.9 1.3 reduce_max.18
  11.3 3.6 conditional.1
  13.1 1.0 fusion.1
  17.1 36.1 %all-gather.5 = f32[32,2,16]{2,1,0:T(2,128)S(1)} all-gather(f32[1,2,16]{2,1,0:T(2,128)S(1)} %bitcast.96), channel_id=3, replica_groups=mesh['req'=8,'blk'=32] {'blk'}, dimensions={0}, use_global_device_ids=true | all-gather | bytes 4224 | tf_op jit(solution)/shard_map/all_gather | solution.py:11
  53.2 30.9 %all-gather.4 = f32[32,2,16]{2,1,0:T(2,128)S(1)} all-gather(f32[1,2,16]{2,1,0:T(2,128)} %bitcast.6), channel_id=2, replica_groups=mesh['req'=8,'blk'=32] {'blk'}, dimensions={0}, use_global_device_ids=true | all-gather | bytes 4224 | tf_op jit(solution)/shard_map/all_gather | solution.py:11
  85.4 30.1 %while.19 = (s32[]{:T(128)}, f32[2,16]{1,0:T(2,128)S(1)}, f32[2,16]{1,0:T(2,128)S(1)}, f32[2,16,512]{2,1,0:T(8,128)S(1)}, f32[32,2,16]{2,1,0:T(2,128)S(1)}, /*in...) while((s32[]{:T(128)}, f32[2,16]{1,0:T(2,128)S(1)}, ...), condition=%wide.region_11.12_spmd, body=%wide.region_10.11_spmd.sunk | while | flops 49349 | bytes 198039 | solution.py:16
  115.7 29.1 %all-gather.12.cloned.1.call-done = bf16[16,512,128]{2,1,0:T(8,128)(2,1)} async-done(((bf16[2,512,128]{2,1,0:T(8,128)(2,1)}), bf16[16,512,128]{2,1,0:T(8,128)(2,1)}) %all-gather.12.cloned.1.call-update) | async-done | bytes 2097168 | tf_op jit(solution)/shard_map/all_gather | solution.py:142
  144.8 115.6 %all-gather.14.cloned.1.call-done = bf16[16,128,2048]{2,1,0:T(8,128)(2,1)} async-done(((bf16[2,128,2048]{2,1,0:T(8,128)(2,1)}), bf16[16,128,2048]{2,1,0:T(8,128)(2,1)}) %all-gather.14.cloned.1.call-update) | async-done | bytes 8388624 | tf_op jit(solution)/shard_map/all_gather | solution.py:143
  260.4 5.6 multiply_reduce_fusion
  267.8 324.9 %all-gather.3 = bf16[256,6,64]{2,1,0:T(8,128)(2,1)S(1)} all-gather(bf16[1,6,64]{2,1,0:T(8,128)(2,1)S(1)} %maximum_bitcast_fusion.1), channel_id=1, replica_groups=mesh['req'=8,'blk'=32] {'req','blk'}, dimensions={0}, use_global_device_ids=true | all-gather | bytes 197376 | tf_op jit(solution)/shard_map/all_gather | solution.py:167
  593.5 88.7 %all-gather.18.cloned.1.call-done = bf16[256,6,2048]{2,1,0:T(8,128)(2,1)} async-done(((bf16[1,6,2048]{2,1,0:T(8,128)(2,1)}), bf16[256,6,2048]{2,1,0:T(8,128)(2,1)}) %all-gather.18.cloned.1.call-update) | async-done | bytes 6291472 | tf_op jit(solution)/shard_map/all_gather | solution.py:166
  682.1 11.0 %reshape.96 = bf16[1536,2048]{1,0:T(8,128)(2,1)} reshape(bf16[256,6,2048]{2,1,0:T(8,128)(2,1)} %all-gather.18.cloned.1.call-done) | data formatting | bytes 12582912
  693.2 6.2 fusion.36
  699.4 3.2 fusion.31
  702.6 1.1 dynamic-slice_bitcast_fusion
  704.3 2.5 fusion.21
  706.9 8.1 fusion.49
  715.0 17.8 %copy.59 = f32[256,6,2048]{2,1,0:T(8,128)} copy(f32[256,6,2048]{2,0,1:T(8,128)} %fusion.49) | data formatting | bytes 25165824 | tf_op jit(solution)/shard_map/tr,rnd->tnd/dot_general | solution.py:183
  732.8 15.9 %reshape.77 = f32[1536,2048]{1,0:T(8,128)} reshape(f32[256,6,2048]{2,1,0:T(8,128)} %copy.59) | data formatting | bytes 25165824 | tf_op jit(solution)/shard_map/reshape | solution.py:187
  748.7 11.5 %fusion.19 = f32[1536,2048]{1,0:T(8,128)} fusion(bf16[1536,2048]{1,0:T(8,128)(2,1)} %reshape.96, f32[1536,176]{0,1:T(8,128)} %fusion.36, bf16[2,176,2048]{2,1,0:T(8,128)(2,1)S(1)} %copy-done.6, bf16[2,2048,176]{1,2,0:T(8,128)(2,1)S(1)} %copy-done.7), kind=kOutput, calls=%fused_computation.32 | convolution fusion | flops 2216214528 | bytes 21397504 | tf_op jit(solution)/shard_map/dot_general | solution.py:35
  760.2 17.7 %add_add_fusion = f32[1536,2048]{1,0:T(8,128)} fusion(f32[1536,2048]{1,0:T(8,128)} %reshape.77, f32[1536,2048]{1,0:T(8,128)} %fusion.19, f32[1536]{0:T(1024)S(1)} %get-tuple-element.233, f32[1536]{0:T(1024)S(1)} %get-tuple-element.232, bf16[2,176,2048]{2,1,0:T(8,128)(2,1)S(1)} %copy-done.6, bf16[1536,2048]{1,0:T(8,128)(2,1)} %reshape.96, ...), kind=kOutput, calls=%fused_computation.23 | convolution fusion | flops 2228797440 | bytes 46579712 | tf_op jit(solution)/shard_map/dot_general | solution.py:35
  778.0 288.3 %all-reduce.3.cloned.1.call-done = f32[1536,2048]{1,0:T(8,128)} async-done(((f32[1536,2048]{1,0:T(8,128)}), f32[1536,2048]{1,0:T(8,128)}) %all-reduce.3.cloned.1.call-update) | async-done | bytes 12582928
  1066.3 1.5 fusion.62
  1067.9 1.5 fusion.65
  (156 shorter events, 40.8 us)
Async XLA Ops:
  7.2 3.7 copy-start
  7.2 4.1 copy-start.18
  7.2 4.1 copy-start.3
  7.2 77.3 %all-gather.16.cloned.1.call-start = ((), (), s32[]{:S(2)}) async-start(), calls=%async_computation.2 | async-start | bytes 2162688 | tf_op jit(solution)/shard_map/all_gather | solution.py:11
  14.9 69.3 %copy-start.16 = (bf16[2,576]{1,0:T(2,128)(2,1)S(1)}, bf16[2,576]{1,0:T(2,128)(2,1)}, u32[]{:S(2)}) copy-start(bf16[2,576]{1,0:T(2,128)(2,1)} %param.30) | copy-start | bytes 6916
  14.9 69.4 %copy-start.9 = (bf16[4,2048]{1,0:T(4,128)(2,1)S(1)}, bf16[4,2048]{1,0:T(4,128)(2,1)}, u32[]{:S(2)}) copy-start(bf16[4,2048]{1,0:T(4,128)(2,1)} %param.24) | copy-start | bytes 49156
  14.9 69.5 %copy-start.11 = (f32[2048]{0:T(1024)S(1)}, f32[2048]{0:T(1024)}, u32[]{:S(2)}) copy-start(f32[2048]{0:T(1024)} %param.34) | copy-start | bytes 24580
  15.5 129.3 %all-gather.12.cloned.1.call-start = ((), (), s32[]{:S(2)}) async-start(), calls=%async_computation | async-start | bytes 2359296 | tf_op jit(solution)/shard_map/all_gather | solution.py:142
  16.3 244.1 %copy-start.12 = (bf16[2,2048]{1,0:T(2,128)(2,1)S(1)}, bf16[2,2048]{1,0:T(2,128)(2,1)}, u32[]{:S(2)}) copy-start(bf16[2,2048]{1,0:T(2,128)(2,1)} %param.27) | copy-start | bytes 24580
  16.3 244.1 %all-gather.14.cloned.1.call-start = ((), (), s32[]{:S(2)}) async-start(), calls=%async_computation.1 | async-start | bytes 9437184 | tf_op jit(solution)/shard_map/all_gather | solution.py:143
  17.0 665.1 %all-gather.18.cloned.1.call-start = ((), (), s32[]{:S(2)}) async-start(), calls=%async_computation.3 | async-start | bytes 8421376 | tf_op jit(solution)/shard_map/all_gather | solution.py:166
  115.7 151.1 %copy-start.13 = (f32[4,6]{1,0:T(4,128)S(1)}, f32[4,6]{1,0:T(4,128)}, u32[]{:S(2)}) copy-start(f32[4,6]{1,0:T(4,128)} %param.26) | copy-start | bytes 292
  115.7 151.4 %copy-start.15 = (s32[4,6]{1,0:T(4,128)S(1)}, s32[4,6]{1,0:T(4,128)}, u32[]{:S(2)}) copy-start(s32[4,6]{1,0:T(4,128)} %param.25) | copy-start | bytes 292
  115.7 151.5 %copy-start.14 = (f32[2,6]{1,0:T(2,128)S(1)}, f32[2,6]{1,0:T(2,128)}, u32[]{:S(2)}) copy-start(f32[2,6]{1,0:T(2,128)} %param.33) | copy-start | bytes 148
  115.7 151.8 %copy-start.17 = (s32[2,6]{1,0:T(2,128)S(1)}, s32[2,6]{1,0:T(2,128)}, u32[]{:S(2)}) copy-start(s32[2,6]{1,0:T(2,128)} %param.32) | copy-start | bytes 148
  266.7 799.6 %all-reduce.3.cloned.1.call-start = ((), (), s32[]{:S(2)}) async-start(), calls=%async_computation.4 | async-start | bytes 25165824
  593.4 99.7 %copy-start.19 = (bf16[2,2048,176]{1,2,0:T(8,128)(2,1)S(1)}, bf16[2,2048,176]{1,2,0:T(8,128)(2,1)}, u32[]{:S(2)}) copy-start(bf16[2,2048,176]{1,2,0:T(8,128)(2,1)} %param.38) | copy-start | bytes 4325380
  693.2 6.2 copy-start.2
  699.4 4.4 copy-start.5
  702.6 1.7 copy-start.4
  732.8 15.9 %copy-start.6 = (bf16[2,176,2048]{2,1,0:T(8,128)(2,1)S(1)}, bf16[2,176,2048]{2,1,0:T(8,128)(2,1)}, u32[]{:S(2)}) copy-start(bf16[2,176,2048]{2,1,0:T(8,128)(2,1)} %param.40) | copy-start | bytes 4325380
  732.8 15.9 %copy-start.7 = (bf16[2,2048,176]{1,2,0:T(8,128)(2,1)S(1)}, bf16[2,2048,176]{1,2,0:T(8,128)(2,1)}, u32[]{:S(2)}) copy-start(bf16[2,2048,176]{1,2,0:T(8,128)(2,1)} %param.39) | copy-start | bytes 4325380
  777.9 288.4 %copy-start.10 = (bf16[4,2048]{1,0:T(4,128)(2,1)S(1)}, bf16[4,2048]{1,0:T(4,128)(2,1)}, u32[]{:S(2)}) copy-start(bf16[4,2048]{1,0:T(4,128)(2,1)} %param.24) | copy-start | bytes 49156
  778.0 291.4 %copy-start.1 = (bf16[16,128,512]{2,1,0:T(8,128)(2,1)S(1)}, bf16[16,128,512]{2,1,0:T(8,128)(2,1)}, u32[]{:S(2)}) copy-start(bf16[16,128,512]{2,1,0:T(8,128)(2,1)} %param.35) | copy-start | bytes 6291460
  (1 other events, 0.6 us)
Sparse Core Ops, SparseCore 0:
  15.7 67.0 all-gather.15
  85.4 59.3 all-gather.11
  147.4 112.8 all-gather.13
  266.8 415.2 all-gather.17
  778.1 288.1 all-reduce.2
where the time goes:
time: 1080 us
  waiting for transfers between devices  523 us (48%)
  blocking collectives  392 us (36%)
  matrix products  57.8 us (5%)
  local copies, waits for them, and re-layouts  50.5 us (5%)
  other arithmetic  36.9 us (3%)
  between operations  14.8 us (1%)
    all_gather x1, blocking collectives, local(): lax.all_gather(own_table, ('req', 'blk'), axis=0, tiled=True)  325 us
    unnamed x6, waiting for transfers between devices  290 us
    all_gather x1, waiting for transfers between devices, local(): proj_piece = lax.all_gather(out_proj, 'req', axis=0, tiled=True)  116 us
    all_gather x1, waiting for transfers between devices, local(): lax.all_gather(own_rows, ('req', 'blk'), axis=0, tiled=True)  88.7 us
    all_gather x2, blocking collectives, merged(): gathered = jax.tree.map(lambda a: lax.all_gather(a, axis), part)  67.1 us
    dot_general x3, matrix products, swiglu(): return jnp.dot(hidden, down_w, preferred_element_type=jnp.float32)  31.7 us
    all_gather x1, waiting for transfers between devices, local(): value_piece = lax.all_gather(absorb_value, 'req', axis=0, tiled=True)  29.1 us
    add x31, other arithmetic, merge_parts(): first_part[2] * keep_first[:, :, None]  28.6 us
  transfers between devices with their start and end apart: 5, of which 4 were waited for; matrix products, arithmetic and copies ran while one was open for 3% of the time, Pallas kernels for 0%

commit v1 on v0

--- a/solution.py
+++ b/solution.py
@@ -140,7 +140,9 @@
     ].astype(jnp.float32)
     o_latent = (weighted / denominator[:, :, None]).astype(jnp.bfloat16)
     value_piece = lax.all_gather(absorb_value, "req", axis=0, tiled=True)
-    proj_piece = lax.all_gather(out_proj, "req", axis=0, tiled=True)
+    proj_piece = jnp.concatenate(
+        lax.all_to_all(jnp.stack([out_proj] * lax.axis_size("req")), "req", 0, 0), axis=0
+    )
     head_values = jnp.einsum(
         "ihl,hlv->ihv", o_latent, value_piece, preferred_element_type=jnp.float32
     ).astype(jnp.bfloat16)

time: 1080 us -> 1030 us (0.954)
  waiting for transfers between devices: 523 us -> 450 us
  blocking collectives: 392 us -> 404 us
    all_gather x1 -> x0, waiting for transfers between devices: 116 us -> none  [local(): proj_piece = lax.all_gather(out_proj, 'req', axis=0, tiled=True)]
    all_gather x1, waiting for transfers between devices: 0.02 us -> 42 us  [merged(): gathered = jax.tree.map(lambda a: lax.all_gather(a, axis), part)]
    unnamed x6 -> x5, waiting for transfers between devices: 290 us -> 290 us
  transfers between devices with their start and end apart: 5 -> 5, of which waited for: 4 -> 4; matrix products, arithmetic and copies ran while one was open for 3% -> 4% of each run, Pallas kernels for 0% -> 0%
where the time goes in v1:
time: 1030 us
  waiting for transfers between devices  450 us (44%)
  blocking collectives  404 us (39%)
  matrix products  57.8 us (6%)
  local copies, waits for them, and re-layouts  56 us (5%)
  other arithmetic  36.9 us (4%)
  between operations  14.7 us (1%)
    all_gather x1, blocking collectives, local(): lax.all_gather(own_table, ('req', 'blk'), axis=0, tiled=True)  326 us
    unnamed x5, waiting for transfers between devices  290 us
    all_gather x1, waiting for transfers between devices, local(): lax.all_gather(own_rows, ('req', 'blk'), axis=0, tiled=True)  87.8 us
    all_gather x2, blocking collectives, merged(): gathered = jax.tree.map(lambda a: lax.all_gather(a, axis), part)  77.6 us
    all_gather x1, waiting for transfers between devices, merged(): gathered = jax.tree.map(lambda a: lax.all_gather(a, axis), part)  42 us
    dot_general x3, matrix products, swiglu(): return jnp.dot(hidden, down_w, preferred_element_type=jnp.float32)  31.8 us
    all_gather x1, waiting for transfers between devices, local(): value_piece = lax.all_gather(absorb_value, 'req', axis=0, tiled=True)  30.2 us
    add x31, other arithmetic, merge_parts(): first_part[2] * keep_first[:, :, None]  28.6 us
  transfers between devices with their start and end apart: 5, of which 4 were waited for; matrix products, arithmetic and copies ran while one was open for 4% of the time, Pallas kernels for 0%

profile of v1, /device:TPU:8, one launch (start us, length us, event | category | flops | bytes accessed | tf_op | source)
XLA Modules:
  0.0 1025.2 jit_solution(18023135501450310412)
XLA Ops:
  8.9 1.3 reduce_max.18
  11.3 3.6 conditional.1
  15.6 5.5 stack.2
  21.1 5.1 all-to-all-start
  27.0 39.9 %all-gather.5 = f32[32,2,16]{2,1,0:T(2,128)S(1)} all-gather(f32[1,2,16]{2,1,0:T(2,128)S(1)} %bitcast.97), channel_id=3, replica_groups=mesh['req'=8,'blk'=32] {'blk'}, dimensions={0}, use_global_device_ids=true | all-gather | bytes 4224 | tf_op jit(solution)/shard_map/all_gather | solution.py:11
  66.9 37.7 %all-gather.4 = f32[32,2,16]{2,1,0:T(2,128)S(1)} all-gather(f32[1,2,16]{2,1,0:T(2,128)} %bitcast.6), channel_id=2, replica_groups=mesh['req'=8,'blk'=32] {'blk'}, dimensions={0}, use_global_device_ids=true | all-gather | bytes 4224 | tf_op jit(solution)/shard_map/all_gather | solution.py:11
  104.9 42.0 %all-gather.13.cloned.1.call-done = f32[64,16,512]{2,1,0:T(8,128)} async-done(((f32[2,16,512]{2,1,0:T(8,128)}), f32[64,16,512]{2,1,0:T(8,128)}) %all-gather.13.cloned.1.call-update) | async-done | bytes 2097168 | tf_op jit(solution)/shard_map/all_gather | solution.py:11
  147.8 30.1 %while.19 = (s32[]{:T(128)}, f32[2,16]{1,0:T(2,128)S(1)}, f32[2,16]{1,0:T(2,128)S(1)}, f32[2,16,512]{2,1,0:T(8,128)S(1)}, f32[32,2,16]{2,1,0:T(2,128)S(1)}, /*in...) while((s32[]{:T(128)}, f32[2,16]{1,0:T(2,128)S(1)}, ...), condition=%wide.region_11.12_spmd, body=%wide.region_10.11_spmd.sunk | while | flops 49349 | bytes 198039 | solution.py:16
  178.1 30.2 %all-gather.11.cloned.1.call-done = bf16[16,512,128]{2,1,0:T(8,128)(2,1)} async-done(((bf16[2,512,128]{2,1,0:T(8,128)(2,1)}), bf16[16,512,128]{2,1,0:T(8,128)(2,1)}) %all-gather.11.cloned.1.call-update) | async-done | bytes 2097168 | tf_op jit(solution)/shard_map/all_gather | solution.py:142
  208.3 5.6 multiply_reduce_fusion
  215.7 326.4 %all-gather.3 = bf16[256,6,64]{2,1,0:T(8,128)(2,1)S(1)} all-gather(bf16[1,6,64]{2,1,0:T(8,128)(2,1)S(1)} %maximum_bitcast_fusion.1), channel_id=1, replica_groups=mesh['req'=8,'blk'=32] {'req','blk'}, dimensions={0}, use_global_device_ids=true | all-gather | bytes 197376 | tf_op jit(solution)/shard_map/all_gather | solution.py:169
  543.0 87.8 %all-gather.15.cloned.1.call-done = bf16[256,6,2048]{2,1,0:T(8,128)(2,1)} async-done(((bf16[1,6,2048]{2,1,0:T(8,128)(2,1)}), bf16[256,6,2048]{2,1,0:T(8,128)(2,1)}) %all-gather.15.cloned.1.call-update) | async-done | bytes 6291472 | tf_op jit(solution)/shard_map/all_gather | solution.py:168
  630.8 11.0 %reshape.102 = bf16[1536,2048]{1,0:T(8,128)(2,1)} reshape(bf16[256,6,2048]{2,1,0:T(8,128)(2,1)} %all-gather.15.cloned.1.call-done) | data formatting | bytes 12582912
  641.8 6.2 fusion.36
  648.0 3.2 fusion.31
  653.0 2.5 fusion.21
  655.6 8.0 fusion.49
  663.6 17.9 %copy.59 = f32[256,6,2048]{2,1,0:T(8,128)} copy(f32[256,6,2048]{2,0,1:T(8,128)} %fusion.49) | data formatting | bytes 25165824 | tf_op jit(solution)/shard_map/tr,rnd->tnd/dot_general | solution.py:185
  681.5 15.9 %reshape.83 = f32[1536,2048]{1,0:T(8,128)} reshape(f32[256,6,2048]{2,1,0:T(8,128)} %copy.59) | data formatting | bytes 25165824 | tf_op jit(solution)/shard_map/reshape | solution.py:189
  697.3 11.5 %fusion.19 = f32[1536,2048]{1,0:T(8,128)} fusion(bf16[1536,2048]{1,0:T(8,128)(2,1)} %reshape.102, f32[1536,176]{0,1:T(8,128)} %fusion.36, bf16[2,176,2048]{2,1,0:T(8,128)(2,1)S(1)} %copy-done.6, bf16[2,2048,176]{1,2,0:T(8,128)(2,1)S(1)} %copy-done.7), kind=kOutput, calls=%fused_computation.32 | convolution fusion | flops 2216214528 | bytes 21397504 | tf_op jit(solution)/shard_map/dot_general | solution.py:35
  708.8 17.8 %add_add_fusion = f32[1536,2048]{1,0:T(8,128)} fusion(f32[1536,2048]{1,0:T(8,128)} %reshape.83, f32[1536,2048]{1,0:T(8,128)} %fusion.19, f32[1536]{0:T(1024)S(1)} %get-tuple-element.233, f32[1536]{0:T(1024)S(1)} %get-tuple-element.232, bf16[2,176,2048]{2,1,0:T(8,128)(2,1)S(1)} %copy-done.6, bf16[1536,2048]{1,0:T(8,128)(2,1)} %reshape.102, ...), kind=kOutput, calls=%fused_computation.23 | convolution fusion | flops 2228797440 | bytes 46579712 | tf_op jit(solution)/shard_map/dot_general | solution.py:35
  726.6 288.9 %all-reduce.3.cloned.1.call-done = f32[1536,2048]{1,0:T(8,128)} async-done(((f32[1536,2048]{1,0:T(8,128)}), f32[1536,2048]{1,0:T(8,128)}) %all-reduce.3.cloned.1.call-update) | async-done | bytes 12582928
  1015.6 1.5 fusion.62
  1017.1 1.5 fusion.65
  (156 shorter events, 42.2 us)
Async XLA Ops:
  7.2 3.7 copy-start
  7.2 4.1 copy-start.18
  7.2 4.1 copy-start.3
  7.2 139.8 %all-gather.13.cloned.1.call-start = ((), (), s32[]{:S(2)}) async-start(), calls=%async_computation.2 | async-start | bytes 2162688 | tf_op jit(solution)/shard_map/all_gather | solution.py:11
  21.1 83.5 %copy-start.16 = (bf16[2,576]{1,0:T(2,128)(2,1)S(1)}, bf16[2,576]{1,0:T(2,128)(2,1)}, u32[]{:S(2)}) copy-start(bf16[2,576]{1,0:T(2,128)(2,1)} %param.30) | copy-start | bytes 6916
  21.1 83.6 %copy-start.9 = (bf16[4,2048]{1,0:T(4,128)(2,1)S(1)}, bf16[4,2048]{1,0:T(4,128)(2,1)}, u32[]{:S(2)}) copy-start(bf16[4,2048]{1,0:T(4,128)(2,1)} %param.24) | copy-start | bytes 49156
  21.1 83.8 %copy-start.11 = (f32[2048]{0:T(1024)S(1)}, f32[2048]{0:T(1024)}, u32[]{:S(2)}) copy-start(f32[2048]{0:T(1024)} %param.34) | copy-start | bytes 24580
  21.1 187.2 %all-to-all-start = ((bf16[8,2,128,2048]{3,2,1,0:T(8,128)(2,1)}), bf16[8,2,128,2048]{3,2,1,0:T(8,128)(2,1)}, u32[]{:S(2)}, u32[]{:S(2)}) async-start(bf16[8,2,128,2048]{3,2,1,0:T(8,128)(2,1)} %stack.2), calls=%async_computation | async-start | bytes 16777216 | tf_op jit(solution)/shard_map/all_to_all | solution.py:144
  26.2 182.1 %copy-start.12 = (bf16[2,2048]{1,0:T(2,128)(2,1)S(1)}, bf16[2,2048]{1,0:T(2,128)(2,1)}, u32[]{:S(2)}) copy-start(bf16[2,2048]{1,0:T(2,128)(2,1)} %param.27) | copy-start | bytes 24580
  26.2 182.1 %all-gather.11.cloned.1.call-start = ((), (), s32[]{:S(2)}) async-start(), calls=%async_computation.1 | async-start | bytes 2359296 | tf_op jit(solution)/shard_map/all_gather | solution.py:142
  26.9 603.8 %all-gather.15.cloned.1.call-start = ((), (), s32[]{:S(2)}) async-start(), calls=%async_computation.3 | async-start | bytes 8421376 | tf_op jit(solution)/shard_map/all_gather | solution.py:168
  208.2 6.5 copy-start.13
  208.2 6.8 copy-start.15
  208.3 6.9 copy-start.14
  208.3 7.1 copy-start.17
  214.7 800.9 %all-reduce.3.cloned.1.call-start = ((), (), s32[]{:S(2)}) async-start(), calls=%async_computation.4 | async-start | bytes 25165824
  543.0 98.8 %copy-start.19 = (bf16[2,2048,176]{1,2,0:T(8,128)(2,1)S(1)}, bf16[2,2048,176]{1,2,0:T(8,128)(2,1)}, u32[]{:S(2)}) copy-start(bf16[2,2048,176]{1,2,0:T(8,128)(2,1)} %param.38) | copy-start | bytes 4325380
  641.8 6.2 copy-start.2
  648.0 4.4 copy-start.5
  651.2 1.7 copy-start.4
  681.4 15.9 %copy-start.6 = (bf16[2,176,2048]{2,1,0:T(8,128)(2,1)S(1)}, bf16[2,176,2048]{2,1,0:T(8,128)(2,1)}, u32[]{:S(2)}) copy-start(bf16[2,176,2048]{2,1,0:T(8,128)(2,1)} %param.40) | copy-start | bytes 4325380
  681.4 15.9 %copy-start.7 = (bf16[2,2048,176]{1,2,0:T(8,128)(2,1)S(1)}, bf16[2,2048,176]{1,2,0:T(8,128)(2,1)}, u32[]{:S(2)}) copy-start(bf16[2,2048,176]{1,2,0:T(8,128)(2,1)} %param.39) | copy-start | bytes 4325380
  726.6 289.0 %copy-start.10 = (bf16[4,2048]{1,0:T(4,128)(2,1)S(1)}, bf16[4,2048]{1,0:T(4,128)(2,1)}, u32[]{:S(2)}) copy-start(bf16[4,2048]{1,0:T(4,128)(2,1)} %param.24) | copy-start | bytes 49156
  726.6 292.0 %copy-start.1 = (bf16[16,128,512]{2,1,0:T(8,128)(2,1)S(1)}, bf16[16,128,512]{2,1,0:T(8,128)(2,1)}, u32[]{:S(2)}) copy-start(bf16[16,128,512]{2,1,0:T(8,128)(2,1)} %param.35) | copy-start | bytes 6291460
  (1 other events, 0.6 us)
Sparse Core Ops, SparseCore 0:
  15.7 131.2 all-gather.12
  149.6 58.6 all-gather.10
  214.8 415.9 all-gather.14
  726.7 288.7 all-reduce.2
